TPU v7x, 32 devices: a whole 2x2x4 slice. The times are simulated.
32 devices in a mesh: groups: 2 (over x), tile: 8 (over z, y), freq: 2 (over core).
Axes of the slice: x: 2, y: 2, z: 4, core: 2. Of those that a mesh axis runs over, the one named last changes fastest.
Arguments:
- panels: bfloat16 [8, 2, 256, 384], P('freq'), may hold values from -0.3125 to 0.3125
- snapshots: bfloat16 [16, 2, 32, 256], P(('groups', 'freq')), parts along dimension 0, may hold values from -6 to 6
- wavenumbers: float32 [8, 384], P('freq'), may hold values from 0.05 to 0.5
- mode_counts: int32 [8], P('freq'), may hold values from 48 to 384, as said below
- mode_mask: int32 [8, 3, 64], P('freq'), may hold values from 0 to 1, as said below
- mode_shapes: bfloat16 [8, 2048, 384], P('freq', 'tile'), may hold values from -6 to 6
Outputs:
- surface: float32 [32, 2048], P(('groups', 'tile', 'freq')), parts along dimension 0
There are 2 independent parts, one for each index of `groups`. A program takes and returns all parts, laid end to end along the dimension named above; an argument that names none is the same for every part. Nothing has to cross between parts.
Inputs may be any that keep to these rules, and one draw needn't show every extreme that they name: `mode_counts`: some frequency has exactly 384 modes and some exactly 48. `mode_mask`: mode block 0 is live in every depth block of every frequency.
All inputs are finite; a program needn't handle non-finite values.
Results may differ from a plain program's by a relative error of at most 0.0005.
Values may be sent and summed in bfloat16 or wider, within the bound.
No kernel may reach another device: no remote copies, remote signals or barrier semaphores. Data moves between devices by JAX's collectives and lax.ppermute only.
A program may use at most 64 MiB of HBM per device.

v0:
```python
import jax
import jax.numpy as jnp
from jax import lax
from jax.sharding import PartitionSpec as P

MBLK = 128
ZBLK = 32
RANGE_DEV = 1
range_anchor = 1000.0
range_step = 25.0


def block_power(
    shapes, first_range, range_count, panels, snapshots, wavenumbers, mode_counts, mode_mask
):
    depth_count = shapes.shape[1]
    modes = shapes.shape[2]
    receivers = panels.shape[2]
    snap_count = snapshots.shape[2]
    block_count = mode_mask.shape[2]
    depth_index = jnp.arange(depth_count, dtype=jnp.int32)
    depth_onehot = (
        depth_index[:, None] // ZBLK == jnp.arange(block_count, dtype=jnp.int32)[None, :]
    ).astype(jnp.float32)
    distances = range_anchor + range_step * (
        first_range + jnp.arange(range_count, dtype=jnp.int32)
    ).astype(jnp.float32)
    mode_index = jnp.arange(modes, dtype=jnp.int32)

    def one_freq(totals, inputs):
        shape_rows, panel_pair, snap_pair, wavenumber, mode_count, live_blocks = inputs
        depth_live = jnp.dot(depth_onehot, live_blocks.astype(jnp.float32).T)
        live_modes = (
            jnp.repeat(depth_live, MBLK, axis=1)
            * (mode_index < mode_count).astype(jnp.float32)[None, :]
        )
        shaped = shape_rows.astype(jnp.float32) * live_modes
        phases = distances[:, None] * wavenumber[None, :]
        real_part = (jnp.cos(phases)[:, None, :] * shaped[None, :, :]).reshape(-1, modes)
        imag_part = (jnp.sin(phases)[:, None, :] * shaped[None, :, :]).reshape(-1, modes)
        mode_terms = jnp.concatenate([real_part, imag_part], axis=1).astype(jnp.bfloat16)
        stacked = jnp.concatenate(
            [
                jnp.concatenate([panel_pair[0], -panel_pair[1]], axis=1),
                jnp.concatenate([panel_pair[1], panel_pair[0]], axis=1),
            ],
            axis=0,
        )
        replica = lax.dot_general(
            mode_terms, stacked, (((1,), (1,)), ((), ())), preferred_element_type=jnp.float32
        ).astype(jnp.bfloat16)
        widened = replica.astype(jnp.float32)
        energy = jnp.sum(widened * widened, axis=1) / receivers + 1e-06
        probing = jnp.concatenate(
            [
                jnp.concatenate([snap_pair[0], snap_pair[1]], axis=1),
                jnp.concatenate([-snap_pair[1], snap_pair[0]], axis=1),
            ],
            axis=0,
        )
        projected = lax.dot_general(
            replica, probing, (((1,), (1,)), ((), ())), preferred_element_type=jnp.float32
        )
        received = jnp.sum(projected * projected, axis=1) / snap_count
        bartlett = (received / (2.0 * receivers * energy)).reshape(range_count, depth_count)
        return (totals + bartlett, None)

    start_totals = jnp.zeros((range_count, depth_count), jnp.float32)
    totals, _ = lax.scan(
        one_freq, start_totals, (shapes, panels, snapshots, wavenumbers, mode_counts, mode_mask)
    )
    return totals


def sum_freqs(partial_value, all_freqs):
    return lax.psum_scatter(partial_value, "freq", scatter_dimension=0, tiled=True) / all_freqs


def on_device(panels, snapshots, wavenumbers, mode_counts, mode_mask, mode_shapes):
    freq_count = lax.axis_size("freq")
    all_freqs = panels.shape[0] * freq_count
    tile_index = lax.axis_index("tile")
    first_range = tile_index * freq_count * RANGE_DEV
    group_ranges = freq_count * RANGE_DEV
    partial_value = block_power(
        lax.all_gather(mode_shapes, "tile", axis=1, tiled=True),
        first_range,
        group_ranges,
        panels,
        snapshots,
        wavenumbers,
        mode_counts,
        mode_mask,
    )
    surface = sum_freqs(partial_value, all_freqs)
    return surface


def solution(mesh):
    in_specs = (
        P("freq", None, None, None),
        P(("groups", "freq"), None, None, None),
        P("freq", None),
        P("freq"),
        P("freq", None, None),
        P("freq", "tile", None),
    )
    out_specs = P(("groups", "tile", "freq"), None)
    return jax.shard_map(
        on_device, mesh=mesh, in_specs=in_specs, out_specs=out_specs, check_vma=False
    )
```

profile of v0, /device:TPU:0, one launch (start us, length us, event | category | flops | bytes accessed | tf_op | source)
XLA Modules:
  0.0 213.4 jit_solution(17028583751913681123)
XLA Ops:
  6.5 2.3 %copy.12 = bf16[4,256,384]{1,2,0:T(8,128)(2,1)} copy(bf16[4,256,384]{2,1,0:T(8,128)(2,1)} %param.13) | data formatting | bytes 1572864 | tf_op args[5]
  8.9 1.3 dynamic-slice
  10.2 101.9 %all-gather.2.cloned.1.call-done = bf16[4,2048,384]{1,2,0:T(8,128)(2,1)} async-done(((bf16[4,256,384]{1,2,0:T(8,128)(2,1)}), bf16[4,2048,384]{1,2,0:T(8,128)(2,1)}) %all-gather.2.cloned.1.call-update) | async-done | bytes 6291472 | tf_op jit(solution)/shard_map/all_gather | solution.py:86
  112.1 89.9 %while.11 = (s32[]{:T(128)}, f32[2,2048]{1,0:T(2,128)S(1)}, f32[4,384]{1,0:T(4,128)}, bf16[4,2048,384]{1,2,0:T(8,128)(2,1)}, s32[4,3,64]{2,0,1:T(4,128)}, /*inde...) while((s32[]{:T(128)}, f32[2,2048]{1,0:T(2,128)S(1)}, ...), condition=%wide.region_3.4_spmd.clone, body=%wide.region_0.3_spmd.clone.sunk | while | flops 3524392704 | bytes 37074904 | solution.py:69
  113.2 1.2 dynamic_slice.42
  115.0 1.8 fusion.59
  116.8 2.4 %copy.22 = f32[2048,384]{1,0:T(8,128)} copy(f32[2048,384]{0,1:T(8,128)S(1)} %bitcast.45) | data formatting | bytes 6291456 | tf_op jit(solution)/shard_map/while/body/eval_jaxpr/mul | solution.py:39
  120.1 4.7 %multiply_convert_fusion.3 = (bf16[2,2048,384]{2,1,0:T(8,128)(2,1)S(1)}, bf16[2,2048,384]{2,1,0:T(8,128)(2,1)}) fusion(f32[2048,384]{1,0:T(8,128)} %copy.22, f32[2,384]{1,0:T(2,128)S(1)} %get-tuple-element.227, f32[2,384]{1,0:T(2,128)S(1)} %get-tuple-element.228), kind=kLoop, calls=%fused_computation.9.clone.1 | loop fusion | flops 6291456 | bytes 9443328 | tf_op jit(solution)/shard_map/convert.3
  126.7 5.4 %multiply_reduce_fusion.2 = (f32[4096]{0:T(1024)S(1)}, bf16[4096,512]{0,1:T(8,128)(2,1)S(1)}) fusion(bf16[256,384]{1,0:T(8,128)(2,1)S(1)} %dynamic-slice_bitcast_fusion.8, bf16[256,384]{1,0:T(8,128)(2,1)S(1)} %get-tuple-element.225, bf16[256,384]{1,0:T(8,128)(2,1)S(1)} %get-tuple-element.226, bf16[4096,384]{1,0:T(8,128)(2,1)} %bitcast.47, ...), kind=kOutput, calls=%fused_computation.3.clone.1 | convolution fusion | flops 3245338624 | bytes 11091968 | tf_op jit(solution)/shard_map/while/body/eval_jaxpr/dot_general | solution.py:49
  135.7 1.2 dynamic_slice.42
  137.5 1.8 fusion.59
  139.3 2.4 %copy.22 = f32[2048,384]{1,0:T(8,128)} copy(f32[2048,384]{0,1:T(8,128)S(1)} %bitcast.45) | data formatting | bytes 6291456 | tf_op jit(solution)/shard_map/while/body/eval_jaxpr/mul | solution.py:39
  142.6 4.7 %multiply_convert_fusion.3 = (bf16[2,2048,384]{2,1,0:T(8,128)(2,1)S(1)}, bf16[2,2048,384]{2,1,0:T(8,128)(2,1)}) fusion(f32[2048,384]{1,0:T(8,128)} %copy.22, f32[2,384]{1,0:T(2,128)S(1)} %get-tuple-element.227, f32[2,384]{1,0:T(2,128)S(1)} %get-tuple-element.228), kind=kLoop, calls=%fused_computation.9.clone.1 | loop fusion | flops 6291456 | bytes 9443328 | tf_op jit(solution)/shard_map/convert.3
  149.2 5.4 %multiply_reduce_fusion.2 = (f32[4096]{0:T(1024)S(1)}, bf16[4096,512]{0,1:T(8,128)(2,1)S(1)}) fusion(bf16[256,384]{1,0:T(8,128)(2,1)S(1)} %dynamic-slice_bitcast_fusion.8, bf16[256,384]{1,0:T(8,128)(2,1)S(1)} %get-tuple-element.225, bf16[256,384]{1,0:T(8,128)(2,1)S(1)} %get-tuple-element.226, bf16[4096,384]{1,0:T(8,128)(2,1)} %bitcast.47, ...), kind=kOutput, calls=%fused_computation.3.clone.1 | convolution fusion | flops 3245338624 | bytes 11091968 | tf_op jit(solution)/shard_map/while/body/eval_jaxpr/dot_general | solution.py:49
  160.0 1.8 fusion.59
  161.8 2.4 %copy.22 = f32[2048,384]{1,0:T(8,128)} copy(f32[2048,384]{0,1:T(8,128)S(1)} %bitcast.45) | data formatting | bytes 6291456 | tf_op jit(solution)/shard_map/while/body/eval_jaxpr/mul | solution.py:39
  165.0 4.7 %multiply_convert_fusion.3 = (bf16[2,2048,384]{2,1,0:T(8,128)(2,1)S(1)}, bf16[2,2048,384]{2,1,0:T(8,128)(2,1)}) fusion(f32[2048,384]{1,0:T(8,128)} %copy.22, f32[2,384]{1,0:T(2,128)S(1)} %get-tuple-element.227, f32[2,384]{1,0:T(2,128)S(1)} %get-tuple-element.228), kind=kLoop, calls=%fused_computation.9.clone.1 | loop fusion | flops 6291456 | bytes 9443328 | tf_op jit(solution)/shard_map/convert.3
  171.7 5.4 %multiply_reduce_fusion.2 = (f32[4096]{0:T(1024)S(1)}, bf16[4096,512]{0,1:T(8,128)(2,1)S(1)}) fusion(bf16[256,384]{1,0:T(8,128)(2,1)S(1)} %dynamic-slice_bitcast_fusion.8, bf16[256,384]{1,0:T(8,128)(2,1)S(1)} %get-tuple-element.225, bf16[256,384]{1,0:T(8,128)(2,1)S(1)} %get-tuple-element.226, bf16[4096,384]{1,0:T(8,128)(2,1)} %bitcast.47, ...), kind=kOutput, calls=%fused_computation.3.clone.1 | convolution fusion | flops 3245338624 | bytes 11091968 | tf_op jit(solution)/shard_map/while/body/eval_jaxpr/dot_general | solution.py:49
  182.5 1.8 fusion.59
  184.3 2.4 %copy.22 = f32[2048,384]{1,0:T(8,128)} copy(f32[2048,384]{0,1:T(8,128)S(1)} %bitcast.45) | data formatting | bytes 6291456 | tf_op jit(solution)/shard_map/while/body/eval_jaxpr/mul | solution.py:39
  187.5 4.7 %multiply_convert_fusion.3 = (bf16[2,2048,384]{2,1,0:T(8,128)(2,1)S(1)}, bf16[2,2048,384]{2,1,0:T(8,128)(2,1)}) fusion(f32[2048,384]{1,0:T(8,128)} %copy.22, f32[2,384]{1,0:T(2,128)S(1)} %get-tuple-element.227, f32[2,384]{1,0:T(2,128)S(1)} %get-tuple-element.228), kind=kLoop, calls=%fused_computation.9.clone.1 | loop fusion | flops 6291456 | bytes 9443328 | tf_op jit(solution)/shard_map/convert.3
  194.1 5.4 %multiply_reduce_fusion.2 = (f32[4096]{0:T(1024)S(1)}, bf16[4096,512]{0,1:T(8,128)(2,1)S(1)}) fusion(bf16[256,384]{1,0:T(8,128)(2,1)S(1)} %dynamic-slice_bitcast_fusion.8, bf16[256,384]{1,0:T(8,128)(2,1)S(1)} %get-tuple-element.225, bf16[256,384]{1,0:T(8,128)(2,1)S(1)} %get-tuple-element.226, bf16[4096,384]{1,0:T(8,128)(2,1)} %bitcast.47, ...), kind=kOutput, calls=%fused_computation.3.clone.1 | convolution fusion | flops 3245338624 | bytes 11091968 | tf_op jit(solution)/shard_map/while/body/eval_jaxpr/dot_general | solution.py:49
  201.9 3.4 %all-reduce = f32[2,2048]{1,0:T(2,128)S(1)} all-reduce(f32[2,2048]{1,0:T(2,128)S(1)} %get-tuple-element.62), channel_id=2, replica_groups=mesh['groups'=2,'tile'=8,'freq'=2] {'freq'}, use_global_device_ids=true, to_apply=%region_4.5.clone | all-reduce | flops 4096 | bytes 32768
  205.3 1.3 dynamic-slice_multiply_fusion
  (62 shorter events, 29.8 us)
Async XLA Ops:
  6.5 105.5 %all-gather.2.cloned.1.call-start = ((), (), s32[]{:S(2)}) async-start(), calls=%async_computation | async-start | bytes 7077888 | tf_op jit(solution)/shard_map/all_gather | solution.py:86
Sparse Core Ops, SparseCore 0:
  9.4 102.6 all-gather.1
where the time goes:
time: 215 us; the launch traced here: 213 us
  waiting for transfers between devices  102 us (47%)
  other arithmetic  37 us (17%)
  local copies, waits for them, and re-layouts  30.6 us (14%)
  matrix products  26.8 us (12%)
  between operations  13.4 us (6%)
  blocking collectives  3.36 us (2%)
    all_gather x1, waiting for transfers between devices, on_device(): lax.all_gather(mode_shapes, 'tile', axis=1, tiled=True)  102 us
    dot_general x4, matrix products, one_freq(): lax.dot_general(mode_terms, stacked, (((1,), (1,)), ((), ())), preferred_...  21.6 us
    another operation x4, other arithmetic  18.8 us
    dynamic_slice x12, local copies, waits for them, and re-layouts, block_power(): lax.scan(one_freq, start_totals, (shapes, panels, snapshots, wavenumbers,...  10.6 us
    mul x4, local copies, waits for them, and re-layouts, one_freq(): jnp.cos(phases)[:, None, :] * shaped[None, :, :]  9.65 us
    mul x4, other arithmetic, one_freq(): shaped = shape_rows.astype(jnp.float32) * live_modes  7.17 us
  transfers between devices with their start and end apart: 1, of which 1 were waited for; matrix products, arithmetic and copies ran while one was open for 1% of the time, Pallas kernels for 0%

commit v1 on v0

--- a/solution.py
+++ b/solution.py
@@ -8,6 +8,19 @@
 RANGE_DEV = 1
 range_anchor = 1000.0
 range_step = 25.0
+
+
+def gather_around(value, axis, dim):
+    ways = lax.axis_size(axis)
+    up = [(d, (d + 1) % ways) for d in range(ways)]
+    down = [(d, (d - 1) % ways) for d in range(ways)]
+    earlier, later = ([value], [value])
+    for _ in range(ways // 2):
+        earlier.append(lax.ppermute(earlier[-1], axis, up))
+    for _ in range((ways - 1) // 2):
+        later.append(lax.ppermute(later[-1], axis, down))
+    line = jnp.concatenate([*earlier[::-1], *later[1:]], axis=dim)
+    return jnp.roll(line, (lax.axis_index(axis) - ways // 2) * value.shape[dim], axis=dim)
 
 
 def block_power(
@@ -83,7 +96,7 @@
     first_range = tile_index * freq_count * RANGE_DEV
     group_ranges = freq_count * RANGE_DEV
     partial_value = block_power(
-        lax.all_gather(mode_shapes, "tile", axis=1, tiled=True),
+        gather_around(mode_shapes, "tile", 1),
         first_range,
         group_ranges,
         panels,

time: 215 us -> 235 us (1.093)
  starting transfers between devices: 0.01 us -> 48.2 us
  waiting for transfers between devices: 102 us -> 78.3 us
  between operations: 13.4 us -> 0.17 us
  local copies, waits for them, and re-layouts: 30.6 us -> 38.9 us
    all_gather x1 -> x0, waiting for transfers between devices: 102 us -> none  [on_device(): lax.all_gather(mode_shapes, 'tile', axis=1, tiled=True)]
    ppermute x0 -> x7, waiting for transfers between devices: none -> 78.3 us  [the longest x4 78.3 us: gather_around(): earlier.append(lax.ppermute(earlier[-1], axis, up))]
    ppermute x0 -> x7, starting transfers between devices: none -> 48.2 us  [the longest x3 40.1 us: gather_around(): later.append(lax.ppermute(later[-1], axis, down))]
    unnamed x2 -> x19, local copies, waits for them, and re-layouts: 3.6 us -> 11.1 us
    dynamic_slice x0 -> x1, local copies, waits for them, and re-layouts: none -> 3.23 us  [gather_around(): jnp.roll(line, (lax.axis_index(axis) - ways // 2) * value.shape[dim], axi...]
    dynamic_slice x12, local copies, waits for them, and re-layouts: 10.6 us -> 8.11 us  [block_power(): lax.scan(one_freq, start_totals, (shapes, panels, snapshots, wavenumbers,...]
  transfers between devices with their start and end apart: 1 -> 7, of which waited for: 1 -> 4; matrix products, arithmetic and copies ran while one was open for 1% -> 2% of each run, Pallas kernels for 0% -> 0%
where the time goes in v1:
time: 235 us; the launch traced here: 233 us
  waiting for transfers between devices  78.3 us (33%)
  starting transfers between devices  48.2 us (21%)
  local copies, waits for them, and re-layouts  38.9 us (17%)
  other arithmetic  37.3 us (16%)
  matrix products  26.8 us (11%)
  blocking collectives  3.36 us (1%)
    ppermute x4, waiting for transfers between devices, gather_around(): earlier.append(lax.ppermute(earlier[-1], axis, up))  78.3 us
    ppermute x3, starting transfers between devices, gather_around(): later.append(lax.ppermute(later[-1], axis, down))  40.1 us
    dot_general x4, matrix products, one_freq(): lax.dot_general(mode_terms, stacked, (((1,), (1,)), ((), ())), preferred_...  21.6 us
    another operation x4, other arithmetic  18.8 us
    unnamed x19, local copies, waits for them, and re-layouts  11.1 us
    mul x4, local copies, waits for them, and re-layouts, one_freq(): jnp.cos(phases)[:, None, :] * shaped[None, :, :]  9.67 us
    dynamic_slice x12, local copies, waits for them, and re-layouts, block_power(): lax.scan(one_freq, start_totals, (shapes, panels, snapshots, wavenumbers,...  8.11 us
    ppermute x4, starting transfers between devices, gather_around(): earlier.append(lax.ppermute(earlier[-1], axis, up))  8.09 us
  transfers between devices with their start and end apart: 7, of which 4 were waited for; matrix products, arithmetic and copies ran while one was open for 2% of the time, Pallas kernels for 0%

profile of v1, /device:TPU:0, one launch (start us, length us, event | category | flops | bytes accessed | tf_op | source)
XLA Modules:
  0.0 233.4 jit_solution(1820462086421144903)
XLA Ops:
  1.4 3.0 %collective-permute-start = (bf16[4,256,384]{1,2,0:T(8,128)(2,1)S(1)}, bf16[4,256,384]{1,2,0:T(8,128)(2,1)S(1)}, u32[]{:S(2)}, u32[]{:S(2)}) collective-permute-start(bf16[4,256,384]{1,2,0:T(8,128)(2,1)S(1)} %copy.15), channel_id=1, source_target_pairs={{0,2},{2,4},{4,6},{6,8},{8,10},{10,12},{12,14},{14,0},{1,3},{3,5},... | collective-permute-start | bytes 2359304 | tf_op jit(solution)/shard_map/ppermute | solution.py:19
  4.4 20.6 %collective-permute-done = bf16[4,256,384]{1,2,0:T(8,128)(2,1)S(1)} collective-permute-done((bf16[4,256,384]{1,2,0:T(8,128)(2,1)S(1)}, bf16[4,256,384]{1,2,0:T(8,128)(2,1)S(1)}, u32[]{:S(2)}, u32[]{:S(2)}) %collective-permute-start) | collective-permute-done | bytes 786464 | tf_op jit(solution)/shard_map/ppermute | solution.py:19
  25.0 4.7 %collective-permute-start.4 = (bf16[4,256,384]{1,2,0:T(8,128)(2,1)S(1)}, bf16[4,256,384]{1,2,0:T(8,128)(2,1)S(1)}, u32[]{:S(2)}, u32[]{:S(2)}) collective-permute-start(bf16[4,256,384]{1,2,0:T(8,128)(2,1)S(1)} %copy.15), channel_id=1, source_target_pairs={{0,14},{2,0},{4,2},{6,4},{8,6},{10,8},{12,10},{14,12},{1,15},{3,1}... | collective-permute-start | bytes 2359304 | tf_op jit(solution)/shard_map/ppermute | solution.py:21
  29.7 28.7 %collective-permute-done.1 = bf16[4,256,384]{1,2,0:T(8,128)(2,1)S(1)} collective-permute-done((bf16[4,256,384]{1,2,0:T(8,128)(2,1)S(1)}, bf16[4,256,384]{1,2,0:T(8,128)(2,1)S(1)}, u32[]{:S(2)}, u32[]{:S(2)}) %collective-permute-start.1) | collective-permute-done | bytes 786464 | tf_op jit(solution)/shard_map/ppermute | solution.py:19
  58.4 2.5 %collective-permute-start.2 = (bf16[4,256,384]{1,2,0:T(8,128)(2,1)S(1)}, bf16[4,256,384]{1,2,0:T(8,128)(2,1)}, u32[]{:S(2)}, u32[]{:S(2)}) collective-permute-start(bf16[4,256,384]{1,2,0:T(8,128)(2,1)S(1)} %collective-permute-done.1), channel_id=1, source_target_pairs={{0,2},{2,4},{4,6},{6,8},{8,10},{10,12},{12,14},{14,0},{1,3},{3,5},... | collective-permute-start | bytes 2359304 | tf_op jit(solution)/shard_map/ppermute | solution.py:19
  60.9 17.8 %collective-permute-start.5 = (bf16[4,256,384]{1,2,0:T(8,128)(2,1)S(1)}, bf16[4,256,384]{1,2,0:T(8,128)(2,1)}, u32[]{:S(2)}, u32[]{:S(2)}) collective-permute-start(bf16[4,256,384]{1,2,0:T(8,128)(2,1)S(1)} %collective-permute-done.4), channel_id=1, source_target_pairs={{0,14},{2,0},{4,2},{6,4},{8,6},{10,8},{12,10},{14,12},{1,15},{3,1}... | collective-permute-start | bytes 2359304 | tf_op jit(solution)/shard_map/ppermute | solution.py:21
  78.7 14.8 %collective-permute-done.2 = bf16[4,256,384]{1,2,0:T(8,128)(2,1)} collective-permute-done((bf16[4,256,384]{1,2,0:T(8,128)(2,1)S(1)}, bf16[4,256,384]{1,2,0:T(8,128)(2,1)}, u32[]{:S(2)}, u32[]{:S(2)}) %collective-permute-start.2) | collective-permute-done | bytes 786464 | tf_op jit(solution)/shard_map/ppermute | solution.py:19
  93.5 2.6 %collective-permute-start.3 = (bf16[4,256,384]{1,2,0:T(8,128)(2,1)}, bf16[4,256,384]{1,2,0:T(8,128)(2,1)}, u32[]{:S(2)}, u32[]{:S(2)}) collective-permute-start(bf16[4,256,384]{1,2,0:T(8,128)(2,1)} %collective-permute-done.2), channel_id=1, source_target_pairs={{0,2},{2,4},{4,6},{6,8},{8,10},{10,12},{12,14},{14,0},{1,3},{3,5},... | collective-permute-start | bytes 2359304 | tf_op jit(solution)/shard_map/ppermute | solution.py:19
  97.4 17.6 %collective-permute-start.6 = (bf16[4,256,384]{1,2,0:T(8,128)(2,1)}, bf16[4,256,384]{1,2,0:T(8,128)(2,1)S(1)}, u32[]{:S(2)}, u32[]{:S(2)}) collective-permute-start(bf16[4,256,384]{1,2,0:T(8,128)(2,1)} %collective-permute-done.5), channel_id=1, source_target_pairs={{0,14},{2,0},{4,2},{6,4},{8,6},{10,8},{12,10},{14,12},{1,15},{3,1}... | collective-permute-start | bytes 2359304 | tf_op jit(solution)/shard_map/ppermute | solution.py:21
  115.0 14.3 %collective-permute-done.3 = bf16[4,256,384]{1,2,0:T(8,128)(2,1)} collective-permute-done((bf16[4,256,384]{1,2,0:T(8,128)(2,1)}, bf16[4,256,384]{1,2,0:T(8,128)(2,1)}, u32[]{:S(2)}, u32[]{:S(2)}) %collective-permute-start.3) | collective-permute-done | bytes 786464 | tf_op jit(solution)/shard_map/ppermute | solution.py:19
  137.9 3.2 %constant_dynamic-slice_fusion.2 = bf16[4,2048,384]{1,2,0:T(8,128)(2,1)} fusion(bf16[4,4096,384]{1,2,0:T(8,128)(2,1)S(1)} %constant_dynamic-update-slice_fusion, s32[]{:T(128)S(6)} %select_n.24), kind=kLoop, calls=%fused_computation.75 | loop fusion | bytes 12582916 | tf_op jit(solution)/shard_map/jit(_roll_dynamic)/dynamic_slice | solution.py:23
  141.1 87.6 %while.11 = (s32[]{:T(128)}, f32[2,2048]{1,0:T(2,128)S(1)}, f32[4,384]{1,0:T(4,128)}, bf16[4,2048,384]{1,2,0:T(8,128)(2,1)}, s32[4,3,64]{2,0,1:T(4,128)}, /*inde...) while((s32[]{:T(128)}, f32[2,2048]{1,0:T(2,128)S(1)}, ...), condition=%wide.region_3.4_spmd.clone, body=%wide.region_0.3_spmd.clone.sunk | while | flops 3524392704 | bytes 37074904 | solution.py:82
  145.3 2.4 %copy.28 = f32[2048,384]{1,0:T(8,128)} copy(f32[2048,384]{0,1:T(8,128)S(1)} %bitcast.45) | data formatting | bytes 6291456 | tf_op jit(solution)/shard_map/while/body/eval_jaxpr/mul | solution.py:52
  148.6 4.7 %multiply_convert_fusion.3 = (bf16[2,2048,384]{2,1,0:T(8,128)(2,1)S(1)}, bf16[2,2048,384]{2,1,0:T(8,128)(2,1)}) fusion(f32[2048,384]{1,0:T(8,128)} %copy.28, f32[2,384]{1,0:T(2,128)S(1)} %get-tuple-element.227, f32[2,384]{1,0:T(2,128)S(1)} %get-tuple-element.228), kind=kLoop, calls=%fused_computation.9.clone.1 | loop fusion | flops 6291456 | bytes 9443328 | tf_op jit(solution)/shard_map/convert.3
  155.2 5.4 %multiply_reduce_fusion.2 = (f32[4096]{0:T(1024)S(1)}, bf16[4096,512]{0,1:T(8,128)(2,1)S(1)}) fusion(bf16[256,384]{1,0:T(8,128)(2,1)S(1)} %dynamic-slice_bitcast_fusion.8, bf16[256,384]{1,0:T(8,128)(2,1)S(1)} %get-tuple-element.225, bf16[256,384]{1,0:T(8,128)(2,1)S(1)} %get-tuple-element.226, bf16[4096,384]{1,0:T(8,128)(2,1)} %bitcast.47, ...), kind=kOutput, calls=%fused_computation.3.clone.1 | convolution fusion | flops 3245338624 | bytes 11091968 | tf_op jit(solution)/shard_map/while/body/eval_jaxpr/dot_general | solution.py:62
  167.2 2.4 %copy.28 = f32[2048,384]{1,0:T(8,128)} copy(f32[2048,384]{0,1:T(8,128)S(1)} %bitcast.45) | data formatting | bytes 6291456 | tf_op jit(solution)/shard_map/while/body/eval_jaxpr/mul | solution.py:52
  170.5 4.7 %multiply_convert_fusion.3 = (bf16[2,2048,384]{2,1,0:T(8,128)(2,1)S(1)}, bf16[2,2048,384]{2,1,0:T(8,128)(2,1)}) fusion(f32[2048,384]{1,0:T(8,128)} %copy.28, f32[2,384]{1,0:T(2,128)S(1)} %get-tuple-element.227, f32[2,384]{1,0:T(2,128)S(1)} %get-tuple-element.228), kind=kLoop, calls=%fused_computation.9.clone.1 | loop fusion | flops 6291456 | bytes 9443328 | tf_op jit(solution)/shard_map/convert.3
  177.1 5.4 %multiply_reduce_fusion.2 = (f32[4096]{0:T(1024)S(1)}, bf16[4096,512]{0,1:T(8,128)(2,1)S(1)}) fusion(bf16[256,384]{1,0:T(8,128)(2,1)S(1)} %dynamic-slice_bitcast_fusion.8, bf16[256,384]{1,0:T(8,128)(2,1)S(1)} %get-tuple-element.225, bf16[256,384]{1,0:T(8,128)(2,1)S(1)} %get-tuple-element.226, bf16[4096,384]{1,0:T(8,128)(2,1)} %bitcast.47, ...), kind=kOutput, calls=%fused_computation.3.clone.1 | convolution fusion | flops 3245338624 | bytes 11091968 | tf_op jit(solution)/shard_map/while/body/eval_jaxpr/dot_general | solution.py:62
  189.1 2.4 %copy.28 = f32[2048,384]{1,0:T(8,128)} copy(f32[2048,384]{0,1:T(8,128)S(1)} %bitcast.45) | data formatting | bytes 6291456 | tf_op jit(solution)/shard_map/while/body/eval_jaxpr/mul | solution.py:52
  192.4 4.7 %multiply_convert_fusion.3 = (bf16[2,2048,384]{2,1,0:T(8,128)(2,1)S(1)}, bf16[2,2048,384]{2,1,0:T(8,128)(2,1)}) fusion(f32[2048,384]{1,0:T(8,128)} %copy.28, f32[2,384]{1,0:T(2,128)S(1)} %get-tuple-element.227, f32[2,384]{1,0:T(2,128)S(1)} %get-tuple-element.228), kind=kLoop, calls=%fused_computation.9.clone.1 | loop fusion | flops 6291456 | bytes 9443328 | tf_op jit(solution)/shard_map/convert.3
  199.0 5.4 %multiply_reduce_fusion.2 = (f32[4096]{0:T(1024)S(1)}, bf16[4096,512]{0,1:T(8,128)(2,1)S(1)}) fusion(bf16[256,384]{1,0:T(8,128)(2,1)S(1)} %dynamic-slice_bitcast_fusion.8, bf16[256,384]{1,0:T(8,128)(2,1)S(1)} %get-tuple-element.225, bf16[256,384]{1,0:T(8,128)(2,1)S(1)} %get-tuple-element.226, bf16[4096,384]{1,0:T(8,128)(2,1)} %bitcast.47, ...), kind=kOutput, calls=%fused_computation.3.clone.1 | convolution fusion | flops 3245338624 | bytes 11091968 | tf_op jit(solution)/shard_map/while/body/eval_jaxpr/dot_general | solution.py:62
  214.3 4.7 %multiply_convert_fusion.3 = (bf16[2,2048,384]{2,1,0:T(8,128)(2,1)S(1)}, bf16[2,2048,384]{2,1,0:T(8,128)(2,1)}) fusion(f32[2048,384]{1,0:T(8,128)} %copy.28, f32[2,384]{1,0:T(2,128)S(1)} %get-tuple-element.227, f32[2,384]{1,0:T(2,128)S(1)} %get-tuple-element.228), kind=kLoop, calls=%fused_computation.9.clone.1 | loop fusion | flops 6291456 | bytes 9443328 | tf_op jit(solution)/shard_map/convert.3
  220.9 5.4 %multiply_reduce_fusion.2 = (f32[4096]{0:T(1024)S(1)}, bf16[4096,512]{0,1:T(8,128)(2,1)S(1)}) fusion(bf16[256,384]{1,0:T(8,128)(2,1)S(1)} %dynamic-slice_bitcast_fusion.8, bf16[256,384]{1,0:T(8,128)(2,1)S(1)} %get-tuple-element.225, bf16[256,384]{1,0:T(8,128)(2,1)S(1)} %get-tuple-element.226, bf16[4096,384]{1,0:T(8,128)(2,1)} %bitcast.47, ...), kind=kOutput, calls=%fused_computation.3.clone.1 | convolution fusion | flops 3245338624 | bytes 11091968 | tf_op jit(solution)/shard_map/while/body/eval_jaxpr/dot_general | solution.py:62
  228.7 3.4 %all-reduce = f32[2,2048]{1,0:T(2,128)S(1)} all-reduce(f32[2,2048]{1,0:T(2,128)S(1)} %get-tuple-element.62), channel_id=2, replica_groups=mesh['groups'=2,'tile'=8,'freq'=2] {'freq'}, use_global_device_ids=true, to_apply=%region_4.5.clone | all-reduce | flops 4096 | bytes 32768
  (92 shorter events, 52.1 us)
Async XLA Ops:
  1.4 23.6 %collective-permute-start = (bf16[4,256,384]{1,2,0:T(8,128)(2,1)S(1)}, bf16[4,256,384]{1,2,0:T(8,128)(2,1)S(1)}, u32[]{:S(2)}, u32[]{:S(2)}) collective-permute-start(bf16[4,256,384]{1,2,0:T(8,128)(2,1)S(1)} %copy.15), channel_id=1, source_target_pairs={{0,2},{2,4},{4,6},{6,8},{8,10},{10,12},{12,14},{14,0},{1,3},{3,5},... | collective-permute-start | bytes 2359304 | tf_op jit(solution)/shard_map/ppermute | solution.py:19
  25.0 33.4 %collective-permute-start.1 = (bf16[4,256,384]{1,2,0:T(8,128)(2,1)S(1)}, bf16[4,256,384]{1,2,0:T(8,128)(2,1)S(1)}, u32[]{:S(2)}, u32[]{:S(2)}) collective-permute-start(bf16[4,256,384]{1,2,0:T(8,128)(2,1)S(1)} %collective-permute-done), channel_id=1, source_target_pairs={{0,2},{2,4},{4,6},{6,8},{8,10},{10,12},{12,14},{14,0},{1,3},{3,5},... | collective-permute-start | bytes 2359304 | tf_op jit(solution)/shard_map/ppermute | solution.py:19
  25.0 35.9 %collective-permute-start.4 = (bf16[4,256,384]{1,2,0:T(8,128)(2,1)S(1)}, bf16[4,256,384]{1,2,0:T(8,128)(2,1)S(1)}, u32[]{:S(2)}, u32[]{:S(2)}) collective-permute-start(bf16[4,256,384]{1,2,0:T(8,128)(2,1)S(1)} %copy.15), channel_id=1, source_target_pairs={{0,14},{2,0},{4,2},{6,4},{8,6},{10,8},{12,10},{14,12},{1,15},{3,1}... | collective-permute-start | bytes 2359304 | tf_op jit(solution)/shard_map/ppermute | solution.py:21
  58.4 35.1 %collective-permute-start.2 = (bf16[4,256,384]{1,2,0:T(8,128)(2,1)S(1)}, bf16[4,256,384]{1,2,0:T(8,128)(2,1)}, u32[]{:S(2)}, u32[]{:S(2)}) collective-permute-start(bf16[4,256,384]{1,2,0:T(8,128)(2,1)S(1)} %collective-permute-done.1), channel_id=1, source_target_pairs={{0,2},{2,4},{4,6},{6,8},{8,10},{10,12},{12,14},{14,0},{1,3},{3,5},... | collective-permute-start | bytes 2359304 | tf_op jit(solution)/shard_map/ppermute | solution.py:19
  60.9 36.5 %collective-permute-start.5 = (bf16[4,256,384]{1,2,0:T(8,128)(2,1)S(1)}, bf16[4,256,384]{1,2,0:T(8,128)(2,1)}, u32[]{:S(2)}, u32[]{:S(2)}) collective-permute-start(bf16[4,256,384]{1,2,0:T(8,128)(2,1)S(1)} %collective-permute-done.4), channel_id=1, source_target_pairs={{0,14},{2,0},{4,2},{6,4},{8,6},{10,8},{12,10},{14,12},{1,15},{3,1}... | collective-permute-start | bytes 2359304 | tf_op jit(solution)/shard_map/ppermute | solution.py:21
  93.5 35.8 %collective-permute-start.3 = (bf16[4,256,384]{1,2,0:T(8,128)(2,1)}, bf16[4,256,384]{1,2,0:T(8,128)(2,1)}, u32[]{:S(2)}, u32[]{:S(2)}) collective-permute-start(bf16[4,256,384]{1,2,0:T(8,128)(2,1)} %collective-permute-done.2), channel_id=1, source_target_pairs={{0,2},{2,4},{4,6},{6,8},{8,10},{10,12},{12,14},{14,0},{1,3},{3,5},... | collective-permute-start | bytes 2359304 | tf_op jit(solution)/shard_map/ppermute | solution.py:19
  97.4 36.0 %collective-permute-start.6 = (bf16[4,256,384]{1,2,0:T(8,128)(2,1)}, bf16[4,256,384]{1,2,0:T(8,128)(2,1)S(1)}, u32[]{:S(2)}, u32[]{:S(2)}) collective-permute-start(bf16[4,256,384]{1,2,0:T(8,128)(2,1)} %collective-permute-done.5), channel_id=1, source_target_pairs={{0,14},{2,0},{4,2},{6,4},{8,6},{10,8},{12,10},{14,12},{1,15},{3,1}... | collective-permute-start | bytes 2359304 | tf_op jit(solution)/shard_map/ppermute | solution.py:21
  133.6 7.5 %copy-start = (s32[4]{0:T(128)S(1)}, s32[4]{0:T(128)}, u32[]{:S(2)}) copy-start(s32[4]{0:T(128)} %param.11) | copy-start | bytes 52
